TPU v7x, 128 devices: a whole 4x4x4 slice. The times are simulated.
128 devices in a mesh: corpus: 16 (over z, y), fsdp: 2 (over core), tensor: 4 (over x).
Axes of the slice: x: 4, y: 4, z: 4, core: 2. Of those that a mesh axis runs over, the one named last changes fastest.
Arguments:
- queries_in: bfloat16 [4096, 4096], P(('corpus', 'fsdp')), may hold values from -6 to 6
- head_weight: bfloat16 [4096, 4096], P('fsdp', 'tensor'), may hold values from -0.09375 to 0.09375
- passages: bfloat16 [16384, 4096], P('corpus', 'tensor'), may hold values from -0.15625 to 0.15625
- teacher: float32 [4096, 4, 32], P(('corpus', 'fsdp')), may hold values from -250 to 400
- cand_block: int32 [4096, 4], P(('corpus', 'fsdp')), may hold values from 0 to 127, all different within a row; in each aligned block of 128 rows (0 to 127, 128 to 255, ...) at most 6 rows name the same one
- cand_offset: int32 [4096, 4, 32], P(('corpus', 'fsdp')), may hold values from 0 to 127, as said below
- block_slot: int32 [128], replicated, may hold values from 0 to 127, each once
Outputs:
- kl_loss: float32 [4096], P(('corpus', 'fsdp'))
- head_grad: float32 [4096, 4096], P('fsdp', 'tensor')
Inputs may be any that keep to these rules, and one draw needn't show every extreme that they name: `cand_block`: in the rows of one device no block id appears more than 6 times, and some block id appears exactly 6 times there; the 4 ids of one query differ. `cand_offset`: the 32 offsets of one query in one block differ. `block_slot`: each storage position is taken by exactly one block.
All inputs are finite; a program needn't handle non-finite values.
Results may differ from a plain program's by a relative error of at most 0.012.
The roundings to bfloat16 on the way count: a program that leaves them out, or rounds other values in their place, can miss the bound.
Values may be sent and summed in bfloat16 or wider, within the bound.
A program may use at most 128 MiB of HBM per device.

v0:
```python
import jax
import jax.numpy as jnp
from jax import lax
from jax.sharding import PartitionSpec as P

ROWS = 128
MOSTB = 6


def on_device(queries_in, head_weight, passages, teacher, cand_block, cand_offset, block_slot):
    query_rows, model_width = queries_in.shape
    head_cols = head_weight.shape[1]
    per_query = cand_block.shape[1]
    offset_count = cand_offset.shape[2]
    total_blocks = block_slot.shape[0]
    n_corpus = lax.axis_size("corpus")
    blocks_here = passages.shape[0] // ROWS
    capacity = MOSTB
    slot_total = total_blocks * capacity
    columns = queries_in
    query = jnp.dot(
        columns,
        lax.all_gather(head_weight, "fsdp", axis=0, tiled=True),
        preferred_element_type=jnp.float32,
    ).astype(jnp.bfloat16)
    block_ids = lax.broadcasted_iota(jnp.int32, (1, total_blocks), 1)
    named = (cand_block.reshape(-1, 1) == block_ids).astype(jnp.int32)
    slot_of = jnp.sum(named * block_slot.reshape(1, -1), axis=1)
    slot_hits = (slot_of[:, None] == block_ids).astype(jnp.int32)
    slot_rank = jnp.sum((jnp.cumsum(slot_hits, axis=0) - slot_hits) * slot_hits, axis=1)
    position = slot_of * capacity + slot_rank
    query_copies = jnp.repeat(query, per_query, axis=0)
    send_queries = jnp.zeros((slot_total, head_cols), jnp.bfloat16).at[position].set(query_copies)
    send_queries = send_queries.reshape(n_corpus, blocks_here, capacity, head_cols)
    offset_rows = cand_offset.reshape(-1, offset_count)
    send_offsets = jnp.zeros((slot_total, offset_count), jnp.int32).at[position].set(offset_rows)
    send_offsets = send_offsets.reshape(n_corpus, blocks_here, capacity, offset_count)
    embedded = passages.reshape(blocks_here, ROWS, head_cols)
    scores = jnp.einsum(
        "sjmd,jrd->sjmr",
        lax.all_to_all(send_queries, "corpus", split_axis=0, concat_axis=0, tiled=True),
        embedded,
        preferred_element_type=jnp.float32,
    )
    returned_scores = lax.all_to_all(scores, "corpus", split_axis=0, concat_axis=0, tiled=True)
    picked = returned_scores.reshape(slot_total, ROWS)[position].reshape(
        query_rows, per_query, ROWS
    )
    partial_scores = jnp.take_along_axis(picked, cand_offset, axis=2)
    student = 50.0 * lax.psum(partial_scores, "tensor")
    log_student = student - jax.nn.logsumexp(student, axis=(1, 2), keepdims=True)
    log_teacher = teacher - jax.nn.logsumexp(teacher, axis=(1, 2), keepdims=True)
    prob_teacher = jnp.exp(log_teacher)
    kl_loss = jnp.sum(prob_teacher * (log_teacher - log_student), axis=(1, 2))
    dscore = (50.0 * (jnp.exp(log_student) - prob_teacher)).astype(jnp.bfloat16)
    flat_index = (position[:, None] * ROWS + offset_rows).reshape(-1)
    dense_grad = (
        jnp.zeros((slot_total * ROWS,), jnp.bfloat16).at[flat_index].set(dscore.reshape(-1))
    )
    dense_grad = dense_grad.reshape(n_corpus, blocks_here, capacity, ROWS)
    block_part = jnp.einsum(
        "sjmr,jrd->sjmd",
        lax.all_to_all(dense_grad, "corpus", split_axis=0, concat_axis=0, tiled=True),
        embedded,
        preferred_element_type=jnp.float32,
    ).astype(jnp.bfloat16)
    arrived_parts = lax.all_to_all(block_part, "corpus", split_axis=0, concat_axis=0, tiled=True)
    parts = arrived_parts.reshape(slot_total, head_cols)[position].reshape(
        query_rows, per_query, head_cols
    )
    query_grad = jnp.sum(parts.astype(jnp.float32), axis=1).astype(jnp.bfloat16)
    columns = queries_in
    grad_share = lax.psum_scatter(
        lax.dot_general(
            columns, query_grad, (((0,), (0,)), ((), ())), preferred_element_type=jnp.float32
        ),
        "fsdp",
        scatter_dimension=0,
        tiled=True,
    )
    head_grad = lax.psum(grad_share, "corpus")
    return (kl_loss, head_grad)


def solution(mesh):
    placed = (
        P(("corpus", "fsdp"), None),
        P("fsdp", "tensor"),
        P("corpus", "tensor"),
        P(("corpus", "fsdp"), None, None),
        P(("corpus", "fsdp"), None),
        P(("corpus", "fsdp"), None, None),
        P(),
    )
    return jax.shard_map(
        on_device,
        mesh=mesh,
        in_specs=placed,
        out_specs=(P(("corpus", "fsdp")), P("fsdp", "tensor")),
        check_vma=False,
    )
```

profile of v0, /device:TPU:1, one launch (start us, length us, event | category | flops | bytes accessed | tf_op | source)
XLA Modules:
  0.0 657.2 jit_solution(10483691207682673269)
XLA Ops:
  10.5 25.5 %all-gather.2.cloned.1.call-done = bf16[4096,1024]{1,0:T(8,128)(2,1)} async-done(((bf16[2048,1024]{1,0:T(8,128)(2,1)}), bf16[4096,1024]{1,0:T(8,128)(2,1)}) %all-gather.2.cloned.1.call-update) | async-done | bytes 8388624 | tf_op jit(solution)/shard_map/all_gather | solution.py:23
  35.9 4.6 convolution_convert_fusion.1
  42.0 4.5 scatter_custom_fusion
  46.5 3.7 reshape.158
  50.2 3.8 copy.62
  54.0 6.8 %all-to-all-start = ((bf16[16,8,6,1024]{3,1,2,0:T(8,128)(2,1)}), bf16[16,8,6,1024]{3,1,2,0:T(8,128)(2,1)}, u32[]{:S(2)}, u32[]{:S(2)}) async-start(bf16[16,8,6,1024]{3,1,2,0:T(8,128)(2,1)} %copy.62), calls=%async_computation | async-start | bytes 3145728 | tf_op jit(solution)/shard_map/all_to_all | solution.py:41
  61.6 24.0 %all-to-all-done = bf16[16,8,6,1024]{3,1,2,0:T(8,128)(2,1)} async-done(((bf16[16,8,6,1024]{3,1,2,0:T(8,128)(2,1)}), bf16[16,8,6,1024]{3,1,2,0:T(8,128)(2,1)}, u32[]{:S(2)}, u32[]{:S(2)}) %all-to-all-start) | async-done | bytes 1572896 | tf_op jit(solution)/shard_map/all_to_all | solution.py:41
  85.6 2.6 fusion.3
  89.2 3.6 all-to-all-start.1
  93.3 8.4 %all-to-all-done.1 = f32[16,8,6,128]{3,1,2,0:T(8,128)S(1)} async-done(((f32[16,8,6,128]{3,1,2,0:T(8,128)}), f32[16,8,6,128]{3,1,2,0:T(8,128)S(1)}, u32[]{:S(2)}, u32[]{:S(2)}) %all-to-all-start.1) | async-done | bytes 393248 | tf_op jit(solution)/shard_map/all_to_all | solution.py:45
  103.0 145.8 %gather_fusion.2 = f32[16384]{0:T(1024)S(1)} fusion(f32[128,4,128]{2,1,0:T(4,128)S(1)} %bitcast.43, s32[16384]{0:T(1024)S(1)} %reshape.184), kind=kCustom, calls=%fused_computation.2 | custom fusion | bytes 327680 | tf_op jit(solution)/shard_map/jit(take_along_axis)/gather | solution.py:49
  250.0 37.5 %all-reduce.3.cloned.1.call-done = f32[128,4,32]{0,2,1:T(8,128)} async-done(((f32[128,4,32]{0,2,1:T(8,128)}), f32[128,4,32]{0,2,1:T(8,128)}) %all-reduce.3.cloned.1.call-update) | async-done | bytes 65552 | tf_op jit(solution)/shard_map/psum | solution.py:50
  291.0 112.7 %scatter_custom_fusion.1 = bf16[98304]{0:T(1024)(128)(2,1)S(1)} fusion(s32[16384]{0:T(1024)} %bitcast.46, bf16[16384]{0:T(1024)(128)(2,1)S(1)} %reshape.202, bf16[]{:T(256)} %constant.17.clone.1), kind=kCustom, calls=%fused_computation.28 | custom fusion | bytes 197120 | tf_op jit(solution)/shard_map/scatter | solution.py:58
  403.8 13.7 %all_to_all.20 = bf16[16,8,6,128]{3,1,2,0:T(8,128)(2,1)S(1)} all-to-all(bf16[16,8,6,128]{3,1,2,0:T(8,128)(2,1)S(1)} %copy.70), channel_id=1, replica_groups=mesh['corpus'=16,'fsdp'=2,'tensor'=4] {'corpus'}, dimensions={0} | all-to-all | bytes 393216 | tf_op jit(solution)/shard_map/all_to_all | solution.py:63
  418.9 21.4 %all_to_all.21 = bf16[16,8,6,1024]{3,1,2,0:T(8,128)(2,1)S(1)} all-to-all(bf16[16,8,6,1024]{3,1,2,0:T(8,128)(2,1)S(1)} %copy.72), channel_id=1, replica_groups=mesh['corpus'=16,'fsdp'=2,'tensor'=4] {'corpus'}, dimensions={0} | all-to-all | bytes 3145728 | tf_op jit(solution)/shard_map/all_to_all | solution.py:67
  440.4 2.4 copy.73
  442.8 3.7 reshape.166
  446.5 5.1 gather_fusion.1
  451.6 2.3 reshape.167
  453.9 2.5 reduce_sum.62
  456.4 8.1 %convolution_bitcast_fusion = f32[4096,1024]{0,1:T(8,128)} fusion(bf16[128,1024]{1,0:T(8,128)(2,1)S(1)} %reduce_sum.62, bf16[128,4096]{1,0:T(8,128)(2,1)S(1)} %copy-done.2), kind=kOutput, calls=%fused_computation.5 | convolution fusion | flops 1073741824 | bytes 18087936 | tf_op jit(solution)/shard_map/dot_general | solution.py:74
  464.6 31.0 %reduce-scatter.2.cloned.1.call-done = f32[2048,1024]{0,1:T(8,128)} async-done(((f32[4096,1024]{0,1:T(8,128)}), f32[2048,1024]{0,1:T(8,128)}) %reduce-scatter.2.cloned.1.call-update) | async-done | bytes 8388624 | tf_op jit(solution)/shard_map/reduce_scatter | solution.py:73
  495.6 145.8 %all-reduce.5.cloned.1.call-done = f32[2048,1024]{0,1:T(8,128)} async-done(((f32[2048,1024]{0,1:T(8,128)}), f32[2048,1024]{0,1:T(8,128)}) %all-reduce.5.cloned.1.call-update) | async-done | bytes 8388624 | tf_op jit(solution)/shard_map/psum | solution.py:81
  641.4 9.2 %copy.74 = f32[2048,1024]{1,0:T(8,128)} copy(f32[2048,1024]{0,1:T(8,128)} %all-reduce.5.cloned.1.call-done) | data formatting | bytes 16777216
  (71 shorter events, 14.2 us)
Async XLA Ops:
  7.2 78.4 %copy-start = (bf16[1024,1024]{1,0:T(8,128)(2,1)S(1)}, bf16[1024,1024]{1,0:T(8,128)(2,1)}, u32[]{:S(2)}) copy-start(bf16[1024,1024]{1,0:T(8,128)(2,1)} %param.9) | copy-start | bytes 6291460
  7.2 0.8 copy-start.6
  7.2 1.0 copy-start.7
  7.2 2.3 copy-start.3
  7.2 28.7 %copy-start.1 = (bf16[128,4096]{1,0:T(8,128)(2,1)S(1)}, bf16[128,4096]{1,0:T(8,128)(2,1)}, u32[]{:S(2)}) copy-start(bf16[128,4096]{1,0:T(8,128)(2,1)} %param.7) | copy-start | bytes 3145732
  7.2 28.7 %all-gather.2.cloned.1.call-start = ((), (), s32[]{:S(2)}) async-start(), calls=%async_computation.5 | async-start | bytes 12582912 | tf_op jit(solution)/shard_map/all_gather | solution.py:23
  50.2 10.7 %copy-start.5 = (s32[16384,1]{0,1:T(1,128)S(1)}, s32[16384,1]{0,1:T(1,128)}, u32[]{:S(2)}) copy-start(s32[16384,1]{0,1:T(1,128)} %reshape.163) | copy-start | bytes 196612
  54.0 31.6 %all-to-all-start = ((bf16[16,8,6,1024]{3,1,2,0:T(8,128)(2,1)}), bf16[16,8,6,1024]{3,1,2,0:T(8,128)(2,1)}, u32[]{:S(2)}, u32[]{:S(2)}) async-start(bf16[16,8,6,1024]{3,1,2,0:T(8,128)(2,1)} %copy.62), calls=%async_computation | async-start | bytes 3145728 | tf_op jit(solution)/shard_map/all_to_all | solution.py:41
  85.6 7.7 %copy-start.4 = (f32[128,4,32]{0,2,1:T(8,128)S(1)}, f32[128,4,32]{0,2,1:T(8,128)}, u32[]{:S(2)}) copy-start(f32[128,4,32]{0,2,1:T(8,128)} %param.10) | copy-start | bytes 196612
  89.2 12.6 %all-to-all-start.1 = ((f32[16,8,6,128]{3,1,2,0:T(8,128)}), f32[16,8,6,128]{3,1,2,0:T(8,128)S(1)}, u32[]{:S(2)}, u32[]{:S(2)}) async-start(f32[16,8,6,128]{3,1,2,0:T(8,128)} %copy.64), calls=%async_computation.1 | async-start | bytes 786432 | tf_op jit(solution)/shard_map/all_to_all | solution.py:45
  92.8 194.7 %all-reduce.3.cloned.1.call-start = ((), (), s32[]{:S(2)}) async-start(), calls=%async_computation.6 | async-start | bytes 131072 | tf_op jit(solution)/shard_map/psum | solution.py:50
  249.8 245.8 %reduce-scatter.2.cloned.1.call-start = ((), (), s32[]{:S(2)}) async-start(), calls=%async_computation.7 | async-start | bytes 25165824 | tf_op jit(solution)/shard_map/reduce_scatter | solution.py:73
  451.6 4.9 copy-start.2
  464.6 176.9 %all-reduce.5.cloned.1.call-start = ((), (), s32[]{:S(2)}) async-start(), calls=%async_computation.8 | async-start | bytes 16777216 | tf_op jit(solution)/shard_map/psum | solution.py:81
Sparse Core Ops, SparseCore 0:
  9.7 26.1 all-gather.1
  249.9 37.5 all-reduce.2
  464.7 30.8 reduce-scatter.1
  499.1 142.3 all-reduce.4
where the time goes:
time: 658 us; the launch traced here: 657 us
  local copies, waits for them, and re-layouts  300 us (46%)
  waiting for transfers between devices  273 us (41%)
  blocking collectives  35.1 us (5%)
  matrix products  15.9 us (2%)
  between operations  14.1 us (2%)
  starting transfers between devices  10.8 us (2%)
  other arithmetic  7.91 us (1%)
    gather x5, local copies, waits for them, and re-layouts, on_device(): partial_scores = jnp.take_along_axis(picked, cand_offset, axis=2)  146 us
    psum x1, waiting for transfers between devices, on_device(): head_grad = lax.psum(grad_share, 'corpus')  146 us
    scatter x1, local copies, waits for them, and re-layouts, on_device(): jnp.zeros((slot_total * ROWS,), jnp.bfloat16).at[flat_index]  113 us
    psum x1, waiting for transfers between devices, on_device(): student = 50.0 * lax.psum(partial_scores, 'tensor')  37.5 us
    reduce_scatter x1, waiting for transfers between devices, on_device(): lax.psum_scatter(lax.dot_general(columns, query_grad, (((0,), (0,)), ((),...  31 us
    all_gather x1, waiting for transfers between devices, on_device(): lax.all_gather(head_weight, 'fsdp', axis=0, tiled=True)  25.5 us
    all_to_all x1, waiting for transfers between devices, on_device(): lax.all_to_all(send_queries, 'corpus', split_axis=0, concat_axis=0, tiled...  24 us
    all_to_all x1, blocking collectives, on_device(): lax.all_to_all(block_part, 'corpus', split_axis=0, concat_axis=0, tiled=T...  21.4 us
  transfers between devices with their start and end apart: 6, of which 6 were waited for; matrix products, arithmetic and copies ran while one was open for 1% of the time, Pallas kernels for 0%

commit v1 on v0

v1 whole, which is shorter than its diff:
```python
import functools
import jax
import jax.numpy as jnp
from jax import lax
from jax.experimental import pallas as pl
from jax.experimental.pallas import tpu as pltpu
from jax.sharding import PartitionSpec as P

BF = jnp.bfloat16
F32 = jnp.float32
I32 = jnp.int32
ROWS = 128
CAP = 6
SIDE = 4
SLOTS = 48
ALL = 768
LANES = 128
MESH = pl.DeviceIdType.MESH


def dot(a, b, dims=((1,), (0,))):
    return lax.dot_general(a, b, (dims, ((), ())), preferred_element_type=F32)


def lane_pick(values, index):
    return jnp.take_along_axis(values, index, axis=1)


def step_kernel(x_hbm, w_hbm, p_hbm, teacher_ref, offs_ref, cand_ref, bslot_ref,
                kl_ref, hg_ref,
                xcat, xt, w, p, part_own, part_send, part_recv, q,
                pmt, pm, r, rt, inv,
                qs, qr, ss, sr, s3, st, ds, dr, dexp, ps, pr, qg2,
                gsend, grecv, gown, hsend, hrecv,
                loc_sem, fs_send, fs_recv, aa_send, aa_recv, te_send, te_recv,
                ar_send, ar_recv):
    c = lax.axis_index("corpus")
    f = lax.axis_index("fsdp")
    t = lax.axis_index("tensor")
    z = lax.div(c, SIDE)
    y = lax.rem(c, SIDE)

    def load(src, dst, k):
        return pltpu.make_async_copy(src, dst, loc_sem.at[k])

    own_cols = pl.ds(pl.multiple_of(f * 2048, 2048), 2048)
    other_cols = pl.ds(pl.multiple_of((1 - f) * 2048, 2048), 2048)
    load_x = load(x_hbm.at[:, own_cols], xcat.at[pl.ds(0, 128), :], 0)
    load_w = load(w_hbm, w, 1)
    load_p = load(p_hbm, p, 2)
    load_x.start()
    load_w.start()
    load_p.start()

    barrier = pltpu.get_barrier_semaphore()

    def peer(dz, dy):
        return lax.rem(z + dz, SIDE) * SIDE + lax.rem(y + dy, SIDE)

    def source(dz, dy):
        return lax.rem(z + SIDE - dz, SIDE) * SIDE + lax.rem(y + SIDE - dy, SIDE)

    pl.semaphore_signal(barrier, inc=1, device_id={"fsdp": 1 - f}, device_id_type=MESH)

    @pl.loop(1, 4)
    def _(i):
        pl.semaphore_signal(
            barrier, inc=1, device_id={"tensor": lax.rem(t + i, 4)}, device_id_type=MESH)

    @pl.loop(1, 16)
    def _(i):
        pl.semaphore_signal(
            barrier, inc=1, device_id={"corpus": peer(lax.div(i, SIDE), lax.rem(i, SIDE))},
            device_id_type=MESH)

    pl.semaphore_wait(barrier, 19)

    swap_x = pltpu.make_async_remote_copy(
        src_ref=x_hbm.at[:, other_cols], dst_ref=xcat.at[pl.ds(128, 128), :],
        send_sem=fs_send.at[0], recv_sem=fs_recv.at[0],
        device_id={"fsdp": 1 - f}, device_id_type=MESH)
    swap_x.start()

    lane = lax.broadcasted_iota(I32, (128, LANES), 1)
    row = lax.broadcasted_iota(I32, (128, LANES), 0)
    slot_row = bslot_ref[...].astype(F32)
    hits = jnp.zeros((128, LANES), F32)
    slots = []
    for g in range(4):
        named = cand_ref[:, g:g + 1] == lane
        slot = jnp.sum(jnp.where(named, slot_row, 0.0), axis=1, keepdims=True).astype(I32)
        slots.append(slot)
        hits = hits + jnp.where(slot == lane, 1.0, 0.0)
    earlier = jnp.where(lane < row, 1.0, 0.0).astype(BF)
    before = dot(earlier, hits.astype(BF))
    place_lane = lax.broadcasted_iota(I32, (128, ALL), 1)
    total = jnp.zeros((128, ALL), F32)
    for g in range(4):
        rank = jnp.sum(jnp.where(slots[g] == lane, before, 0.0), axis=1, keepdims=True).astype(I32)
        place = (slots[g] >> 3) * SLOTS + rank * 8 + (slots[g] & 7)
        one = jnp.where(place == place_lane, 1.0, 0.0)
        total = total + one
        pmt[g, :, :] = one.astype(BF)
        pm[:, g * 128:(g + 1) * 128] = one.T.astype(BF)
    rt[...] = total.astype(BF)
    r[...] = total.T.astype(BF)

    load_x.wait()
    load_w.wait()

    @pl.loop(0, 4)
    def _(n):
        cols = pl.ds(pl.multiple_of(n * 256, 256), 256)
        part_own[:, cols] = dot(xcat[0:128, :], w[:, cols])

    swap_x.wait_recv()

    @pl.loop(0, 4)
    def _(n):
        cols = pl.ds(pl.multiple_of(n * 256, 256), 256)
        part_send[:, cols] = dot(xcat[128:256, :], w[:, cols])

    swap_part = pltpu.make_async_remote_copy(
        src_ref=part_send, dst_ref=part_recv,
        send_sem=fs_send.at[1], recv_sem=fs_recv.at[1],
        device_id={"fsdp": 1 - f}, device_id_type=MESH)
    swap_part.start()
    swap_part.wait_recv()
    q[...] = (part_own[...] + part_recv[...]).astype(BF)

    def out_copy(src, dst, chan, dz, dy):
        to = peer(dz, dy)
        return pltpu.make_async_remote_copy(
            src_ref=src.at[pl.ds(pl.multiple_of(to * SLOTS, 16), SLOTS), :],
            dst_ref=dst.at[pl.ds(pl.multiple_of(c * SLOTS, 16), SLOTS), :],
            send_sem=aa_send.at[chan, dz * SIDE + dy], recv_sem=aa_recv.at[chan, dz * SIDE + dy],
            device_id={"corpus": to}, device_id_type=MESH)

    def in_copy(src, dst, chan, dz, dy):
        frm = source(dz, dy)
        rows = pl.ds(pl.multiple_of(frm * SLOTS, 16), SLOTS)
        return pltpu.make_async_remote_copy(
            src_ref=src.at[rows, :], dst_ref=dst.at[rows, :],
            send_sem=aa_send.at[chan, dz * SIDE + dy], recv_sem=aa_recv.at[chan, dz * SIDE + dy],
            device_id={"corpus": frm}, device_id_type=MESH)

    def start_out(src, dst, chan, dz, dy):
        rows = pl.ds(pl.multiple_of(c * SLOTS, 16), SLOTS)
        off = dz * SIDE + dy

        @pl.when(off == 0)
        def _():
            pltpu.make_async_copy(src.at[rows, :], dst.at[rows, :], aa_recv.at[chan, 0]).start()

        @pl.when(off != 0)
        def _():
            out_copy(src, dst, chan, dz, dy).start()

    def wait_in(src, dst, chan, dz, dy):
        rows = pl.ds(pl.multiple_of(c * SLOTS, 16), SLOTS)
        off = dz * SIDE + dy

        @pl.when(off == 0)
        def _():
            pltpu.make_async_copy(src.at[rows, :], dst.at[rows, :], aa_recv.at[chan, 0]).wait()

        @pl.when(off != 0)
        def _():
            in_copy(src, dst, chan, dz, dy).wait_recv()

    @pl.loop(0, 16)
    def _(i):
        n = 15 - i
        dz, dy = lax.div(n, SIDE), lax.rem(n, SIDE)
        to = peer(dz, dy)
        rows = pl.ds(pl.multiple_of(to * SLOTS, 16), SLOTS)
        qs[rows, :] = dot(r[rows, :], q[...]).astype(BF)
        start_out(qs, qr, 0, dz, dy)

    offs = offs_ref[...]
    for g in range(4):
        inv[g, :, :] = jnp.full((128, LANES), -1, I32)

    @pl.loop(0, 32)
    def _(k):
        for g in range(4):
            at = jnp.full((128, LANES), g * 32, I32) + k
            here = lane_pick(offs, at)
            inv[g, :, :] = jnp.where(here == lane, at, inv[g, :, :])

    @pl.loop(0, 8)
    def _(n):
        cols = pl.ds(pl.multiple_of(n * 256, 256), 256)
        xt[cols, :] = xcat[:, cols].T

    load_p.wait()

    sub = lax.broadcasted_iota(I32, (192, LANES), 0) & 7

    @pl.loop(0, 4)
    def _(k):
        dz = k ^ (k >> 1)
        zs = lax.rem(z + SIDE - dz, SIDE)

        @pl.loop(0, 4)
        def _(dy):
            wait_in(qs, qr, 0, dz, dy)

        rows = pl.ds(pl.multiple_of(zs * 192, 16), 192)
        acc = jnp.zeros((192, LANES), F32)
        for j in range(4):
            both = dot(qr[rows, :], p[j * 256:(j + 1) * 256, :], ((1,), (1,)))
            acc = jnp.where(sub == 2 * j, both[:, :128], acc)
            acc = jnp.where(sub == 2 * j + 1, both[:, 128:], acc)
        ss[rows, :] = acc

        @pl.loop(0, 4)
        def _(dy):
            start_out(ss, sr, 1, lax.rem(SIDE - dz, SIDE), lax.rem(SIDE - dy, SIDE))

    @pl.loop(0, 16)
    def _(i):
        wait_in(ss, sr, 1, lax.div(i, SIDE), lax.rem(i, SIDE))

    back = sr[...]
    s3[:, 0:128] = back.astype(BF)
    back = back - s3[:, 0:128].astype(F32)
    s3[:, 128:256] = back.astype(BF)
    back = back - s3[:, 128:256].astype(F32)
    s3[:, 256:384] = back.astype(BF)
    mine = jnp.zeros((128, LANES), F32)
    for g in range(4):
        three = dot(pmt[g, :, :], s3[...])
        dense = three[:, 0:128] + (three[:, 128:256] + three[:, 256:384])
        mine = jnp.where((lane >> 5) == g, lane_pick(dense, offs), mine)
    st[t, :, :] = mine

    def te_copy(i):
        return pltpu.make_async_remote_copy(
            src_ref=st.at[t], dst_ref=st.at[t],
            send_sem=te_send.at[i], recv_sem=te_recv.at[i],
            device_id={"tensor": lax.rem(t + i, 4)}, device_id_type=MESH)

    def te_in(i):
        frm = lax.rem(t + 4 - i, 4)
        return pltpu.make_async_remote_copy(
            src_ref=st.at[frm], dst_ref=st.at[frm],
            send_sem=te_send.at[i], recv_sem=te_recv.at[i],
            device_id={"tensor": frm}, device_id_type=MESH)

    for i in (2, 1, 3):
        te_copy(i).start()
    teacher = teacher_ref[...]
    teacher_top = jnp.max(teacher, axis=1, keepdims=True)
    teacher_lse = teacher_top + jnp.log(
        jnp.sum(jnp.exp(teacher - teacher_top), axis=1, keepdims=True))
    log_teacher = teacher - teacher_lse
    prob_teacher = jnp.exp(log_teacher)
    for i in (1, 3, 2):
        te_in(i).wait_recv()
    student = 50.0 * (((st[0, :, :] + st[1, :, :]) + st[2, :, :]) + st[3, :, :])
    top = jnp.max(student, axis=1, keepdims=True)
    log_student = student - (top + jnp.log(
        jnp.sum(jnp.exp(student - top), axis=1, keepdims=True)))
    dscore = (50.0 * (jnp.exp(log_student) - prob_teacher)).astype(BF).astype(F32)
    spread = jnp.zeros((ALL, LANES), F32)
    for g in range(4):
        at = inv[g, :, :]
        dense = jnp.where(at >= 0, lane_pick(dscore, jnp.maximum(at, 0)), 0.0)
        spread = spread + dot(pm[:, g * 128:(g + 1) * 128], dense.astype(BF))
    ds[...] = spread.astype(BF)

    @pl.loop(0, 16)
    def _(i):
        n = 15 - i
        start_out(ds, dr, 2, lax.div(n, SIDE), lax.rem(n, SIDE))

    terms = prob_teacher * (log_teacher - log_student)
    kl_ref[...] = jnp.sum(terms.T, axis=0, keepdims=True)

    @pl.loop(0, 4)
    def _(k):
        dz = k ^ (k >> 1)
        zs = lax.rem(z + SIDE - dz, SIDE)

        @pl.loop(0, 4)
        def _(dy):
            wait_in(ds, dr, 2, dz, dy)

        rows = pl.ds(pl.multiple_of(zs * 192, 16), 192)
        given = dr[rows, :].astype(F32)
        for j in range(8):
            dexp[:, j * 128:(j + 1) * 128] = jnp.where(sub == j, given, 0.0).astype(BF)

        @pl.loop(0, 4)
        def _(n):
            cols = pl.ds(pl.multiple_of(n * 256, 256), 256)
            ps[rows, cols] = dot(dexp[...], p[:, cols]).astype(BF)

        @pl.loop(0, 4)
        def _(dy):
            start_out(ps, pr, 3, lax.rem(SIDE - dz, SIDE), lax.rem(SIDE - dy, SIDE))

    @pl.loop(0, 16)
    def _(i):
        wait_in(ps, pr, 3, lax.div(i, SIDE), lax.rem(i, SIDE))

    @pl.loop(0, 4)
    def _(n):
        cols = pl.ds(pl.multiple_of(n * 256, 256), 256)
        qg2[0:128, cols] = dot(rt[...], pr[:, cols]).astype(BF)

    swap_qg = pltpu.make_async_remote_copy(
        src_ref=qg2.at[pl.ds(0, 128), :], dst_ref=qg2.at[pl.ds(128, 128), :],
        send_sem=fs_send.at[2], recv_sem=fs_recv.at[2],
        device_id={"fsdp": 1 - f}, device_id_type=MESH)
    swap_qg.start()
    swap_qg.wait_recv()

    first = (z, y)
    second = (y, z)

    def ring(half, stage):
        along_z = (half == 0) == (stage == 0)
        here = z if along_z else y

        def at(i):
            there = lax.rem(here + i, SIDE)
            dev = there * SIDE + y if along_z else z * SIDE + there
            return there, dev
        return here, at

    def send_piece(half, stage, i, src, dst, sem):
        _, at = ring(half, stage)
        _, dev = at(i)
        return pltpu.make_async_remote_copy(
            src_ref=src, dst_ref=dst,
            send_sem=ar_send.at[sem, half, i - 1], recv_sem=ar_recv.at[sem, half, i - 1],
            device_id={"corpus": dev}, device_id_type=MESH)

    for i in (2, 1, 3, 0):
        for half in range(2):
            here, at = ring(half, 0)
            there, _ = at(i)
            lhs = pl.ds(pl.multiple_of(half * 1024 + there * 256, 256), 256)

            @pl.loop(0, 4)
            def _(n, half=half, there=there, lhs=lhs, i=i):
                cols = pl.ds(pl.multiple_of(n * 256, 256), 256)
                prod = dot(xt[lhs, :], qg2[:, cols])
                if i == 0:
                    gown[half, :, cols] = prod
                else:
                    gsend[half, there, :, cols] = prod.astype(BF)

            if i != 0:
                send_piece(half, 0, i, gsend.at[half, there], grecv.at[half, here], 0).start()

    def frm(half, stage, i):
        here, _ = ring(half, stage)
        return lax.rem(here + SIDE - i, SIDE)

    def wait_piece(half, stage, i, dst, sem):
        send_piece(half, stage, i, dst, dst, sem).wait_recv()

    for half in range(2):
        for i in (1, 3, 2):
            wait_piece(half, 0, i, grecv.at[half, frm(half, 0, i)], 0)
        here0, _ = ring(half, 0)
        here1, at1 = ring(half, 1)
        for i in (2, 1, 3, 0):
            there, _ = at1(i)
            rows = pl.ds(pl.multiple_of(there * 64, 64), 64)
            total = gown[half, rows, :]
            for k in (1, 2, 3):
                total = total + grecv[half, frm(half, 0, k), rows, :].astype(F32)
            if i == 0:
                gown[half, rows, :] = total
            else:
                hsend[half, there, :, :] = total.astype(BF)
                send_piece(half, 1, i, hsend.at[half, there], hrecv.at[half, here1], 1).start()

    def out_rows(half, a, b):
        return pl.ds(pl.multiple_of(half * 1024 + a * 256 + b * 64, 64), 64)

    def out_quarter(half, a):
        return pl.ds(pl.multiple_of(half * 1024 + a * 256, 256), 256)

    for half in range(2):
        for i in (1, 3, 2):
            wait_piece(half, 1, i, hrecv.at[half, frm(half, 1, i)], 1)
        here0, _ = ring(half, 0)
        here1, _ = ring(half, 1)
        total = gown[half, pl.ds(pl.multiple_of(here1 * 64, 64), 64), :]
        for k in (1, 2, 3):
            total = total + hrecv[half, frm(half, 1, k), :, :].astype(F32)
        mine_rows = out_rows(half, here0, here1)
        hg_ref[mine_rows, :] = total.astype(BF)
        for i in (2, 1, 3):
            send_piece(half, 1, i, hg_ref.at[mine_rows, :], hg_ref.at[mine_rows, :], 2).start()

    for half in range(2):
        here0, _ = ring(half, 0)
        for i in (1, 3, 2):
            wait_piece(half, 1, i, hg_ref.at[out_rows(half, here0, frm(half, 1, i)), :], 2)
        quarter = out_quarter(half, here0)
        for i in (2, 1, 3):
            send_piece(half, 0, i, hg_ref.at[quarter, :], hg_ref.at[quarter, :], 3).start()

    for half in range(2):
        for i in (1, 3, 2):
            wait_piece(half, 0, i, hg_ref.at[out_quarter(half, frm(half, 0, i)), :], 3)

    swap_x.wait_send()
    swap_part.wait_send()
    swap_qg.wait_send()
    for i in (1, 2, 3):
        te_copy(i).wait_send()
    for chan, (src, dst) in enumerate(((qs, qr), (ss, sr), (ds, dr), (ps, pr))):
        @pl.loop(1, 16)
        def _(n, chan=chan, src=src, dst=dst):
            out_copy(src, dst, chan, lax.div(n, SIDE), lax.rem(n, SIDE)).wait_send()
    for half in range(2):
        here0, at0 = ring(half, 0)
        here1, at1 = ring(half, 1)
        mine_rows = out_rows(half, here0, here1)
        quarter = out_quarter(half, here0)
        for i in (1, 2, 3):
            send_piece(half, 0, i, gsend.at[half, at0(i)[0]], grecv.at[half, here0], 0).wait_send()
            send_piece(half, 1, i, hsend.at[half, at1(i)[0]], hrecv.at[half, here1], 1).wait_send()
            send_piece(half, 1, i, hg_ref.at[mine_rows, :], hg_ref.at[mine_rows, :], 2).wait_send()
            send_piece(half, 0, i, hg_ref.at[quarter, :], hg_ref.at[quarter, :], 3).wait_send()


def on_device(queries_in, head_weight, passages, teacher, cand_block, cand_offset, block_slot):
    vmem = pl.BlockSpec(memory_space=pltpu.VMEM)
    anywhere = pl.BlockSpec(memory_space=pl.ANY)
    V = pltpu.VMEM
    dma = pltpu.SemaphoreType.DMA
    kl, hg = pl.pallas_call(
        step_kernel,
        out_shape=(jax.ShapeDtypeStruct((1, 128), F32), jax.ShapeDtypeStruct((2048, 1024), BF)),
        in_specs=[anywhere, anywhere, anywhere, vmem, vmem, vmem, vmem],
        out_specs=(vmem, vmem),
        scratch_shapes=[
            V((256, 2048), BF), V((2048, 256), BF), V((2048, 1024), BF), V((1024, 1024), BF),
            V((128, 1024), F32), V((128, 1024), F32), V((128, 1024), F32), V((128, 1024), BF),
            V((4, 128, ALL), BF), V((ALL, 512), BF), V((ALL, 128), BF), V((128, ALL), BF),
            V((4, 128, LANES), I32),
            V((ALL, 1024), BF), V((ALL, 1024), BF), V((ALL, LANES), F32), V((ALL, LANES), F32),
            V((ALL, 384), BF), V((4, 128, LANES), F32), V((ALL, LANES), BF), V((ALL, LANES), BF),
            V((192, 1024), BF), V((ALL, 1024), BF), V((ALL, 1024), BF), V((256, 1024), BF),
            V((2, 4, 256, 1024), BF), V((2, 4, 256, 1024), BF), V((2, 256, 1024), F32),
            V((2, 4, 64, 1024), BF), V((2, 4, 64, 1024), BF),
            dma((3,)), dma((3,)), dma((3,)), dma((4, 16)), dma((4, 16)), dma((4,)), dma((4,)),
            dma((4, 2, 3)), dma((4, 2, 3)),
        ],
        compiler_params=pltpu.CompilerParams(
            collective_id=0, has_side_effects=True, vmem_limit_bytes=56 * 1024 * 1024),
    )(queries_in, head_weight, passages, teacher.reshape(128, 128), cand_offset.reshape(128, 128),
      cand_block, block_slot.reshape(1, 128))
    return kl.reshape(128), hg.astype(F32)


def solution(mesh):
    placed = (
        P(("corpus", "fsdp"), None),
        P("fsdp", "tensor"),
        P("corpus", "tensor"),
        P(("corpus", "fsdp"), None, None),
        P(("corpus", "fsdp"), None),
        P(("corpus", "fsdp"), None, None),
        P(),
    )
    return jax.shard_map(
        on_device,
        mesh=mesh,
        in_specs=placed,
        out_specs=(P(("corpus", "fsdp")), P("fsdp", "tensor")),
        check_vma=False,
    )
```

time: 658 us -> 168 us (0.26)
  local copies, waits for them, and re-layouts: 300 us -> 5.06 us
  waiting for transfers between devices: 273 us -> 0 us
  Pallas kernels: 0 us -> 156 us
  blocking collectives: 35.1 us -> 0 us
  matrix products: 15.9 us -> 0 us
  between operations: 14.1 us -> 0.65 us
  starting transfers between devices: 10.8 us -> 0 us
    psum x2 -> x0, waiting for transfers between devices: 183 us -> none  [the longest x1 146 us: on_device(): head_grad = lax.psum(grad_share, 'corpus')]
    pallas_call x0 -> x1, Pallas kernels: none -> 156 us  [on_device(): pl.pallas_call(step_kernel, out_shape=(jax.ShapeDtypeStruct((1, 128), F32...]
    gather x7 -> x0, local copies, waits for them, and re-layouts: 153 us -> none  [the longest x5 146 us: on_device(): partial_scores = jnp.take_along_axis(picked, cand_offset, axis=2)]
    scatter x2 -> x0, local copies, waits for them, and re-layouts: 117 us -> none  [the longest x1 113 us: on_device(): jnp.zeros((slot_total * ROWS,), jnp.bfloat16).at[flat_index]]
    all_to_all x2 -> x0, blocking collectives: 35.1 us -> none  [the longest x1 21.4 us: on_device(): lax.all_to_all(block_part, 'corpus', split_axis=0, concat_axis=0, tiled=T...]
    all_to_all x2 -> x0, waiting for transfers between devices: 32.4 us -> none  [the longest x1 24 us: on_device(): lax.all_to_all(send_queries, 'corpus', split_axis=0, concat_axis=0, tiled...]
    reduce_scatter x1 -> x0, waiting for transfers between devices: 31 us -> none  [on_device(): lax.psum_scatter(lax.dot_general(columns, query_grad, (((0,), (0,)), ((),...]
    all_gather x1 -> x0, waiting for transfers between devices: 25.5 us -> none  [on_device(): lax.all_gather(head_weight, 'fsdp', axis=0, tiled=True)]
  transfers between devices with their start and end apart: 6 -> 0, of which waited for: 6 -> 0; matrix products, arithmetic and copies ran while one was open for 1% -> 0% of each run, Pallas kernels for 0% -> 0%
where the time goes in v1:
time: 168 us
  Pallas kernels  156 us (93%)
  other arithmetic  6.63 us (4%)
  local copies, waits for them, and re-layouts  5.06 us (3%)
    pallas_call x1, Pallas kernels, on_device(): pl.pallas_call(step_kernel, out_shape=(jax.ShapeDtypeStruct((1, 128), F32...  156 us
    convert_element_type x1, other arithmetic, on_device(): return (kl.reshape(128), hg.astype(F32))  6.63 us

profile of v1, /device:TPU:1, one launch (start us, length us, event | category | flops | bytes accessed | tf_op | source)
XLA Modules:
  0.0 168.1 jit_solution(10356309413142558824)
XLA Ops:
  0.6 1.6 copy.12.teacher_ref
  2.2 1.4 copy.14.cand_ref
  3.6 1.6 copy.13.offs_ref
  5.2 155.8 %shard_map.86 = (f32[1,128]{1,0:T(1,128)}, bf16[2048,1024]{1,0:T(8,128)(2,1)}) custom-call(bf16[128,4096]{1,0:T(8,128)(2,1)} %x_hbm.1, bf16[2048,1024]{1,0:T(8,128)(2,1)} %w_hbm.1, bf16[1024,1024]{1,0:T(8,128)(2,1)} %p_hbm.1, f32[128,128]{1,0:T(8,128)} %copy.12.teacher_ref, s32[128,128]{1,0:T(8,128)} %copy.13.offs_ref, s32[128,4]{1,0:T(8,128)} %copy.14.cand_ref, ...), custom_call_target="tpu_custom_call" | custom-call | tf_op jit(solution)/shard_map/pallas_call | solution.py:440
  160.9 0.0 copy-start
  161.0 6.6 %convert_element_type.3 = f32[2048,1024]{1,0:T(8,128)} convert(bf16[2048,1024]{1,0:T(8,128)(2,1)} %get-tuple-element.5) | non-fusion elementwise | flops 2097152 | bytes 12582912 | tf_op jit(solution)/shard_map/convert_element_type | solution.py:462
  167.6 0.0 copy-done
  167.6 0.5 copy.16
Async XLA Ops:
  160.9 6.6 %copy-start = (f32[1,128]{1,0:T(1,128)S(1)}, f32[1,128]{1,0:T(1,128)}, u32[]{:S(2)}) copy-start(f32[1,128]{1,0:T(1,128)} %get-tuple-element.4) | copy-start | bytes 1540

commit v2 on v0

v2 whole, which is shorter than its diff:
```python
import jax
import jax.numpy as jnp
from jax import lax
from jax.experimental import pallas as pl
from jax.experimental.pallas import tpu as pltpu
from jax.sharding import PartitionSpec as P

BF = jnp.bfloat16
F32 = jnp.float32
I32 = jnp.int32
SIDE = 4
SLOTS = 48
ALL = 768
LANES = 128
HALF = 512
MESH = pl.DeviceIdType.MESH
FAR = ((2, 2), (1, 2), (2, 1), (3, 2), (2, 3), (1, 1), (3, 3), (1, 3), (3, 1),
       (2, 0), (0, 2), (1, 0), (0, 1), (3, 0), (0, 3), (0, 0))


def dot(a, b, dims=((1,), (0,))):
    return lax.dot_general(a, b, (dims, ((), ())), preferred_element_type=F32)


def lane_pick(values, index):
    return jnp.take_along_axis(values, index, axis=1)


def step_kernel(x_hbm, w_hbm, p_hbm, teacher_ref, offs_ref, cand_ref, bslot_ref,
                kl_ref, hg_ref,
                xcat, xz, xzt, w, p, part_own, part_send, part_recv, q,
                pm, pmt, r, rtz, inv, offs_s,
                qs, qr, ss, sr, s3, dn, st, ds, dr, dexp, ps, pr, qga, qg2, qz,
                gown, hsend, hrecv,
                loc_sem, fs_send, fs_recv, aa_send, aa_recv, te_send, te_recv,
                xb_send, xb_recv, ql_send, ql_recv, qc_send, qc_recv,
                h_send, h_recv, s_send, s_recv, f_send, f_recv):
    c = lax.axis_index("corpus")
    f = lax.axis_index("fsdp")
    t = lax.axis_index("tensor")
    z = lax.div(c, SIDE)
    y = lax.rem(c, SIDE)
    sent = []
    looped = []

    def peer(dz, dy):
        return lax.rem(z + dz, SIDE) * SIDE + lax.rem(y + dy, SIDE)

    def source(dz, dy):
        return lax.rem(z + SIDE - dz, SIDE) * SIDE + lax.rem(y + SIDE - dy, SIDE)

    def half_cols(h):
        return pl.ds(h * HALF, HALF)

    own_cols = pl.ds(pl.multiple_of(f * 2048, 2048), 2048)
    other_cols = pl.ds(pl.multiple_of((1 - f) * 2048, 2048), 2048)
    load_x = pltpu.make_async_copy(
        x_hbm.at[:, own_cols], xcat.at[pl.ds(0, 128), :], loc_sem.at[0])
    load_w = pltpu.make_async_copy(w_hbm, w, loc_sem.at[1])
    load_p = pltpu.make_async_copy(p_hbm, p, loc_sem.at[2])
    load_x.start()
    load_w.start()
    load_p.start()

    barrier = pltpu.get_barrier_semaphore()
    pl.semaphore_signal(barrier, inc=1, device_id={"fsdp": 1 - f}, device_id_type=MESH)

    @pl.loop(1, 4)
    def _(i):
        pl.semaphore_signal(
            barrier, inc=1, device_id={"tensor": lax.rem(t + i, 4)}, device_id_type=MESH)

    @pl.loop(1, 16)
    def _(i):
        pl.semaphore_signal(
            barrier, inc=1, device_id={"corpus": peer(lax.div(i, SIDE), lax.rem(i, SIDE))},
            device_id_type=MESH)

    lane = lax.broadcasted_iota(I32, (128, LANES), 1)
    row = lax.broadcasted_iota(I32, (128, LANES), 0)
    slot_of = jnp.broadcast_to(bslot_ref[...].astype(F32), (128, LANES)).T
    hits = jnp.zeros((128, LANES), F32)
    slots = []
    for g in range(4):
        named = cand_ref[g:g + 1, :] == row
        slot = jnp.sum(jnp.where(named, slot_of, 0.0), axis=0, keepdims=True).astype(I32)
        slots.append(slot)
        hits = hits + jnp.where(slot == row, 1.0, 0.0)
    earlier = jnp.where(row < lane, 1.0, 0.0).astype(BF)
    before = dot(hits.astype(BF), earlier)
    places = []
    for g in range(4):
        rank = jnp.sum(jnp.where(slots[g] == row, before, 0.0), axis=0, keepdims=True).astype(I32)
        places.append((slots[g] >> 3) * SLOTS + rank * 8 + (slots[g] & 7))
    for n in range(4):
        place_row = lax.broadcasted_iota(I32, (192, LANES), 0) + n * 192
        total = jnp.zeros((192, LANES), F32)
        for g in range(4):
            one = jnp.where(places[g] == place_row, 1.0, 0.0)
            total = total + one
            pm[n * 192:(n + 1) * 192, g * 128:(g + 1) * 128] = one.astype(BF)
        r[n * 192:(n + 1) * 192, :] = total.astype(BF)

    pl.semaphore_wait(barrier, 19)

    def fs_copy(src, dst, k):
        return pltpu.make_async_remote_copy(
            src_ref=src, dst_ref=dst, send_sem=fs_send.at[k], recv_sem=fs_recv.at[k],
            device_id={"fsdp": 1 - f}, device_id_type=MESH)

    def begin(copy):
        copy.start()
        sent.append(copy)
        return copy

    swap_x = begin(fs_copy(x_hbm.at[:, other_cols], xcat.at[pl.ds(128, 128), :], 0))

    def view(ref, at, h):
        rows = pl.ds(pl.multiple_of(at * SLOTS, 16), SLOTS)
        return ref.at[rows, :] if h is None else ref.at[rows, half_cols(h)]

    def out_copy(src, dst, chan, h, dz, dy):
        to, k, n = peer(dz, dy), 0 if h is None else h, dz * SIDE + dy
        return pltpu.make_async_remote_copy(
            src_ref=view(src, to, h), dst_ref=view(dst, c, h),
            send_sem=aa_send.at[chan, k, n], recv_sem=aa_recv.at[chan, k, n],
            device_id={"corpus": to}, device_id_type=MESH)

    def in_copy(src, dst, chan, h, dz, dy):
        frm, k, n = source(dz, dy), 0 if h is None else h, dz * SIDE + dy
        return pltpu.make_async_remote_copy(
            src_ref=view(src, frm, h), dst_ref=view(dst, frm, h),
            send_sem=aa_send.at[chan, k, n], recv_sem=aa_recv.at[chan, k, n],
            device_id={"corpus": frm}, device_id_type=MESH)

    def self_copy(src, dst, chan, h):
        return pltpu.make_async_copy(
            view(src, c, h), view(dst, c, h), aa_recv.at[chan, 0 if h is None else h, 0])

    def start_out(src, dst, chan, h, dz, dy):
        off = dz * SIDE + dy

        @pl.when(off == 0)
        def _():
            self_copy(src, dst, chan, h).start()

        @pl.when(off != 0)
        def _():
            out_copy(src, dst, chan, h, dz, dy).start()

    def wait_in(src, dst, chan, h, dz, dy):
        off = dz * SIDE + dy

        @pl.when(off == 0)
        def _():
            self_copy(src, dst, chan, h).wait()

        @pl.when(off != 0)
        def _():
            in_copy(src, dst, chan, h, dz, dy).wait_recv()

    def order(k):
        return (3 - k) ^ ((3 - k) >> 1)

    def wait_group(src, dst, chan, h, dz):
        @pl.loop(0, 4)
        def _(k):
            wait_in(src, dst, chan, h, dz, order(k))

    def group_rows(dz):
        zs = lax.rem(z + SIDE - dz, SIDE)
        return zs, pl.ds(pl.multiple_of(zs * 192, 16), 192)

    def answer_group(src, dst, chan, h, dz):
        @pl.loop(0, 4)
        def _(k):
            start_out(src, dst, chan, h, lax.rem(SIDE - dz, SIDE),
                      lax.rem(SIDE - order(k), SIDE))

    def finish():
        for copy in sent:
            copy.wait_send()
        for src, dst, chan, h in looped:
            @pl.loop(1, 16)
            def _(n, src=src, dst=dst, chan=chan, h=h):
                out_copy(src, dst, chan, h, lax.div(n, SIDE), lax.rem(n, SIDE)).wait_send()

    load_x.wait()
    load_w.wait()

    @pl.loop(0, 4)
    def _(n):
        cols = pl.ds(pl.multiple_of(n * 256, 256), 256)
        part_own[:, cols] = dot(xcat[0:128, :], w[:, cols])

    swap_x.wait_recv()
    swaps = []
    for h in range(2):
        @pl.loop(2 * h, 2 * h + 2)
        def _(n):
            cols = pl.ds(pl.multiple_of(n * 256, 256), 256)
            part_send[:, cols] = dot(xcat[128:256, :], w[:, cols])

        swaps.append(begin(fs_copy(
            part_send.at[:, half_cols(h)], part_recv.at[:, half_cols(h)], 1 + h)))

    def along(half, stage, i):
        if (half == 0) == (stage == 0):
            there = lax.rem(z + i, SIDE)
            return there, there * SIDE + y
        there = lax.rem(y + i, SIDE)
        return there, z * SIDE + there

    def remote(src, dst, send_sem, recv_sem, dev):
        return pltpu.make_async_remote_copy(
            src_ref=src, dst_ref=dst, send_sem=send_sem, recv_sem=recv_sem,
            device_id={"corpus": dev}, device_id_type=MESH)

    def xb_copy(half, i):
        there, dev = along(half, 0, i)
        cols = pl.ds(pl.multiple_of(half * 1024 + there * 256, 256), 256)
        return remote(xcat.at[:, cols], xz.at[half, i - 1],
                      xb_send.at[half, i - 1], xb_recv.at[half, i - 1], dev)

    for i in (2, 1, 3):
        for half in range(2):
            begin(xb_copy(half, i))

    for h in range(2):
        cols = half_cols(h)
        swaps[h].wait_recv()
        q[:, cols] = (part_own[:, cols] + part_recv[:, cols]).astype(BF)

        @pl.loop(0, 4)
        def _(n, cols=cols):
            rows = pl.ds(pl.multiple_of(n * 192, 16), 192)
            qs[rows, cols] = dot(r[rows, :], q[:, cols]).astype(BF)

        for dz, dy in FAR:
            if (dz, dy) == (0, 0):
                self_copy(qs, qr, 0, h).start()
            else:
                begin(out_copy(qs, qr, 0, h, dz, dy))

    offs = offs_ref[...].astype(F32).T.astype(I32)
    offs_s[...] = offs
    for g in range(4):
        inv[g, :, :] = jnp.full((128, LANES), -1, I32)

    @pl.loop(0, 32)
    def _(k):
        for g in range(4):
            at = jnp.full((128, LANES), g * 32, I32) + k
            here = lane_pick(offs_s[...], at)
            inv[g, :, :] = jnp.where(here == lane, at, inv[g, :, :])

    for n in range(4):
        rows = slice(n * 192, (n + 1) * 192)
        rtz[n, :, :] = r[rows, :].astype(F32).T.astype(BF)
        for g in range(4):
            pmt[n, g * 128:(g + 1) * 128, :] = (
                pm[rows, g * 128:(g + 1) * 128].astype(F32).T.astype(BF))
    dn[...] = jnp.zeros((512, LANES), F32)
    qga[...] = jnp.zeros((128, 1024), F32)

    load_p.wait()
    sub = lax.broadcasted_iota(I32, (192, LANES), 0) & 7
    for h in range(2):
        @pl.loop(0, 4)
        def _(k, h=h):
            dz = order(k)
            zs, rows = group_rows(dz)
            wait_group(qs, qr, 0, h, dz)
            acc = jnp.zeros((192, LANES), F32)
            for j in range(4):
                both = dot(qr[rows, half_cols(h)], p[j * 256:(j + 1) * 256, half_cols(h)],
                           ((1,), (1,)))
                acc = jnp.where(sub == 2 * j, both[:, :128], acc)
                acc = jnp.where(sub == 2 * j + 1, both[:, 128:], acc)
            if h == 0:
                ss[rows, :] = acc
            else:
                ss[rows, :] = ss[rows, :] + acc
                answer_group(ss, sr, 1, None, dz)
    looped.append((ss, sr, 1, None))

    @pl.loop(0, 4)
    def _(k):
        dz = order(k)
        zs, rows = group_rows(dz)
        wait_group(ss, sr, 1, None, dz)
        back = sr[rows, :]
        s3[:, 0:128] = back.astype(BF)
        back = back - s3[:, 0:128].astype(F32)
        s3[:, 128:256] = back.astype(BF)
        back = back - s3[:, 128:256].astype(F32)
        s3[:, 256:384] = back.astype(BF)
        three = dot(pmt[zs, :, :], s3[...])
        dn[...] = dn[...] + (three[:, 0:128] + (three[:, 128:256] + three[:, 256:384]))

    mine = jnp.zeros((128, LANES), F32)
    for g in range(4):
        mine = jnp.where((lane >> 5) == g,
                         lane_pick(dn[g * 128:(g + 1) * 128, :], offs_s[...]), mine)
    st[t, :, :] = mine

    def te_copy(i):
        return pltpu.make_async_remote_copy(
            src_ref=st.at[t], dst_ref=st.at[t],
            send_sem=te_send.at[i], recv_sem=te_recv.at[i],
            device_id={"tensor": lax.rem(t + i, 4)}, device_id_type=MESH)

    def te_in(i):
        frm = lax.rem(t + 4 - i, 4)
        return pltpu.make_async_remote_copy(
            src_ref=st.at[frm], dst_ref=st.at[frm],
            send_sem=te_send.at[i], recv_sem=te_recv.at[i],
            device_id={"tensor": frm}, device_id_type=MESH)

    for i in (2, 1, 3):
        begin(te_copy(i))
    teacher = teacher_ref[...].T
    teacher_top = jnp.max(teacher, axis=1, keepdims=True)
    teacher_lse = teacher_top + jnp.log(
        jnp.sum(jnp.exp(teacher - teacher_top), axis=1, keepdims=True))
    log_teacher = teacher - teacher_lse
    prob_teacher = jnp.exp(log_teacher)
    for i in (1, 3, 2):
        te_in(i).wait_recv()
    student = 50.0 * (((st[0, :, :] + st[1, :, :]) + st[2, :, :]) + st[3, :, :])
    top = jnp.max(student, axis=1, keepdims=True)
    log_student = student - (top + jnp.log(
        jnp.sum(jnp.exp(student - top), axis=1, keepdims=True)))
    dscore = (50.0 * (jnp.exp(log_student) - prob_teacher)).astype(BF).astype(F32)
    for g in range(4):
        at = inv[g, :, :]
        dense = jnp.where(at >= 0, lane_pick(dscore, jnp.maximum(at, 0)), 0.0)
        dexp[g * 128:(g + 1) * 128, 0:128] = dense.astype(BF)

    @pl.loop(0, 4)
    def _(k):
        dz = lax.rem(SIDE - order(k), SIDE)
        zs, rows = group_rows(dz)
        ds[rows, :] = dot(pm[rows, :], dexp[0:512, 0:128]).astype(BF)
        answer_group(ds, dr, 2, None, dz)
    looped.append((ds, dr, 2, None))

    terms = prob_teacher * (log_teacher - log_student)
    kl_ref[...] = jnp.sum(terms.T, axis=0, keepdims=True)

    for h in range(2):
        @pl.loop(0, 4)
        def _(k, h=h):
            dz = order(k)
            zs, rows = group_rows(dz)
            if h == 0:
                wait_group(ds, dr, 2, None, dz)
                given = dr[rows, :].astype(F32)
                for j in range(8):
                    dexp[rows, j * 128:(j + 1) * 128] = jnp.where(sub == j, given, 0.0).astype(BF)

            @pl.loop(2 * h, 2 * h + 2)
            def _(n):
                cols = pl.ds(pl.multiple_of(n * 256, 256), 256)
                ps[rows, cols] = dot(dexp[rows, :], p[:, cols]).astype(BF)

            answer_group(ps, pr, 3, h, dz)
        looped.append((ps, pr, 3, h))

    def wait_recv(dst, send_sem, recv_sem):
        remote(dst, dst, send_sem, recv_sem, lax.rem(c + 1, 16)).wait_recv()

    for half in range(2):
        here, _ = along(half, 0, 0)
        cols = pl.ds(pl.multiple_of(half * 1024 + here * 256, 256), 256)
        xzt[half, 0, :, :] = xcat[:, cols].T
        for i in (1, 3, 2):
            wait_recv(xz.at[half, i - 1], xb_send.at[half, i - 1], xb_recv.at[half, i - 1])
            xzt[half, i, :, :] = xz[half, i - 1, :, :].T

    def ql_copy(src, axis, h, i, slot):
        _, dev = along(axis, 0, i)
        return remote(src, qz.at[axis, slot - 1, pl.ds(0, 128), half_cols(h)],
                      ql_send.at[axis, h, slot - 1], ql_recv.at[axis, h, slot - 1], dev)

    def ql_wait(axis, h, slot):
        wait_recv(qz.at[axis, slot - 1, pl.ds(0, 128), half_cols(h)],
                  ql_send.at[axis, h, slot - 1], ql_recv.at[axis, h, slot - 1])

    def qc_copy(axis, h, slot):
        return pltpu.make_async_remote_copy(
            src_ref=qz.at[axis, slot - 1, pl.ds(0, 128), half_cols(h)],
            dst_ref=qz.at[axis, slot - 1, pl.ds(128, 128), half_cols(h)],
            send_sem=qc_send.at[axis, h, slot - 1], recv_sem=qc_recv.at[axis, h, slot - 1],
            device_id={"fsdp": 1 - f}, device_id_type=MESH)

    swap_q = []
    for h in range(2):
        cols = half_cols(h)

        @pl.loop(0, 4)
        def _(k, h=h, cols=cols):
            dz = order(k)
            zs, rows = group_rows(dz)
            wait_group(ps, pr, 3, h, dz)
            qga[:, cols] = qga[:, cols] + dot(rtz[zs, :, :], pr[rows, cols])

        qg2[0:128, cols] = qga[:, cols].astype(BF)
        mine = qg2.at[pl.ds(0, 128), cols]
        for i, slot in ((1, 1), (3, 3)):
            for axis in range(2):
                begin(ql_copy(mine, axis, h, i, slot))
        swap_q.append(begin(fs_copy(mine, qg2.at[pl.ds(128, 128), cols], 3 + h)))

    for h in range(2):
        on = 1 if h == 0 else 3
        for slot in (on, 4 - on):
            for axis in range(2):
                ql_wait(axis, h, slot)
                if slot == on:
                    begin(ql_copy(qz.at[axis, slot - 1, pl.ds(0, 128), half_cols(h)],
                                  axis, h, on, 2))
                begin(qc_copy(axis, h, slot))

    for h in range(2):
        cols = half_cols(h)
        swap_q[h].wait_recv()
        for half in range(2):
            gown[half, :, cols] = dot(xzt[half, 0, :, :], qg2[:, cols])
        for slot in (1, 3):
            for half in range(2):
                qc_copy(half, h, slot).wait_recv()
                gown[half, :, cols] = gown[half, :, cols] + dot(
                    xzt[half, slot, :, :], qz[half, slot - 1, :, cols])
        for half in range(2):
            ql_wait(half, h, 2)
            begin(qc_copy(half, h, 2))
        for half in range(2):
            qc_copy(half, h, 2).wait_recv()
            gown[half, :, cols] = gown[half, :, cols] + dot(
                xzt[half, 2, :, :], qz[half, 1, :, cols])
            for i in (2, 1, 3):
                there, dev = along(half, 1, i)
                rows = pl.ds(pl.multiple_of(there * 64, 64), 64)
                hsend[half, i - 1, :, cols] = gown[half, rows, cols].astype(BF)
                begin(remote(hsend.at[half, i - 1, :, cols], hrecv.at[half, i - 1, :, cols],
                             h_send.at[half, h, i - 1], h_recv.at[half, h, i - 1], dev))

    def piece(half, h, i, j):
        a, _ = along(half, 0, SIDE - i)
        b, _ = along(half, 1, SIDE - j)
        rows = pl.ds(pl.multiple_of(half * 1024 + a * 256 + b * 64, 64), 64)
        return hg_ref.at[rows, half_cols(h)]

    def second(half, h, j, i, slot):
        ref = piece(half, h, 0, j)
        _, dev = along(half, 1, i)
        begin(remote(ref, ref, s_send.at[half, h, slot - 1], s_recv.at[half, h, slot - 1], dev))

    def second_wait(half, h, slot):
        wait_recv(piece(half, h, 0, slot), s_send.at[half, h, slot - 1],
                  s_recv.at[half, h, slot - 1])

    def first(half, h, j, k, i, slot):
        ref = piece(half, h, k, j)
        _, dev = along(half, 0, i)
        begin(remote(ref, ref, f_send.at[half, h, j, slot - 1],
                     f_recv.at[half, h, j, slot - 1], dev))

    def first_wait(half, h, j, slot):
        wait_recv(piece(half, h, slot, j), f_send.at[half, h, j, slot - 1],
                  f_recv.at[half, h, j, slot - 1])

    both = [(h, half) for h in range(2) for half in range(2)]
    for h, half in both:
        cols = half_cols(h)
        for i in (1, 3, 2):
            wait_recv(hrecv.at[half, i - 1, :, cols], h_send.at[half, h, i - 1],
                      h_recv.at[half, h, i - 1])
        here, _ = along(half, 1, 0)
        total = gown[half, pl.ds(pl.multiple_of(here * 64, 64), 64), cols]
        for i in (1, 2, 3):
            total = total + hrecv[half, i - 1, :, cols].astype(F32)
        a, _ = along(half, 0, 0)
        hg_ref[pl.ds(pl.multiple_of(half * 1024 + a * 256 + here * 64, 64), 64), cols] = (
            total.astype(BF))
        for i in (1, 3):
            second(half, h, 0, i, i)
            first(half, h, 0, 0, i, i)

    for h, half in both:
        on = 1 if h == 0 else 3
        for slot in (on, 4 - on):
            second_wait(half, h, slot)
            if slot == on:
                second(half, h, slot, on, 2)
            for i in (1, 3):
                first(half, h, slot, 0, i, i)

    def pass_on(h, half, j):
        on = 1 if h == 0 else 3
        first_wait(half, h, j, on)
        first(half, h, j, on, on, 2)

    for h, half in both:
        pass_on(h, half, 0)
    for h, half in both:
        second_wait(half, h, 2)
        for i in (1, 3):
            first(half, h, 2, 0, i, i)
    for j in (1, 3, 2):
        for h, half in both:
            pass_on(h, half, j)
    for h, half in both:
        on = 1 if h == 0 else 3
        for j in (0, 1, 3, 2):
            first_wait(half, h, j, 4 - on)
            first_wait(half, h, j, 2)
    finish()


def on_device(queries_in, head_weight, passages, teacher, cand_block, cand_offset, block_slot):
    vmem = pl.BlockSpec(memory_space=pltpu.VMEM)
    anywhere = pl.BlockSpec(memory_space=pl.ANY)
    V = pltpu.VMEM
    dma = pltpu.SemaphoreType.DMA
    kl, hg = pl.pallas_call(
        step_kernel,
        out_shape=(jax.ShapeDtypeStruct((1, 128), F32), jax.ShapeDtypeStruct((2048, 1024), BF)),
        in_specs=[anywhere, anywhere, anywhere, vmem, vmem, vmem, vmem],
        out_specs=(vmem, vmem),
        scratch_shapes=[
            V((256, 2048), BF), V((2, 3, 256, 256), BF), V((2, 4, 256, 256), BF),
            V((2048, 1024), BF), V((1024, 1024), BF),
            V((128, 1024), F32), V((128, 1024), F32), V((128, 1024), F32), V((128, 1024), BF),
            V((ALL, 512), BF), V((4, 512, 192), BF), V((ALL, 128), BF), V((4, 128, 192), BF),
            V((4, 128, LANES), I32), V((128, LANES), I32),
            V((ALL, 1024), BF), V((ALL, 1024), BF), V((ALL, LANES), F32), V((ALL, LANES), F32),
            V((192, 384), BF), V((512, LANES), F32), V((4, 128, LANES), F32),
            V((ALL, LANES), BF), V((ALL, LANES), BF),
            V((ALL, 1024), BF), V((ALL, 1024), BF), V((ALL, 1024), BF),
            V((128, 1024), F32), V((256, 1024), BF), V((2, 3, 256, 1024), BF),
            V((2, 256, 1024), F32), V((2, 3, 64, 1024), BF), V((2, 3, 64, 1024), BF),
            dma((3,)), dma((5,)), dma((5,)), dma((4, 2, 16)), dma((4, 2, 16)),
            dma((4,)), dma((4,)),
            dma((2, 3)), dma((2, 3)), dma((2, 2, 3)), dma((2, 2, 3)), dma((2, 2, 3)),
            dma((2, 2, 3)), dma((2, 2, 3)), dma((2, 2, 3)), dma((2, 2, 3)), dma((2, 2, 3)),
            dma((2, 2, 4, 3)), dma((2, 2, 4, 3)),
        ],
        compiler_params=pltpu.CompilerParams(
            collective_id=0, has_side_effects=True, vmem_limit_bytes=56 * 1024 * 1024),
    )(queries_in, head_weight, passages, teacher.reshape(128, 128).T,
      cand_offset.reshape(128, 128).T, cand_block.T, block_slot.reshape(1, 128))
    return kl.reshape(128), hg.astype(F32)


def solution(mesh):
    placed = (
        P(("corpus", "fsdp"), None),
        P("fsdp", "tensor"),
        P("corpus", "tensor"),
        P(("corpus", "fsdp"), None, None),
        P(("corpus", "fsdp"), None),
        P(("corpus", "fsdp"), None, None),
        P(),
    )
    return jax.shard_map(
        on_device,
        mesh=mesh,
        in_specs=placed,
        out_specs=(P(("corpus", "fsdp")), P("fsdp", "tensor")),
        check_vma=False,
    )
```

time: 658 us -> 129 us (0.20)
  local copies, waits for them, and re-layouts: 300 us -> 0.52 us
  waiting for transfers between devices: 273 us -> 0 us
  Pallas kernels: 0 us -> 121 us
  blocking collectives: 35.1 us -> 0 us
  matrix products: 15.9 us -> 0 us
  between operations: 14.1 us -> 0.65 us
  starting transfers between devices: 10.8 us -> 0 us
    psum x2 -> x0, waiting for transfers between devices: 183 us -> none  [the longest x1 146 us: on_device(): head_grad = lax.psum(grad_share, 'corpus')]
    gather x7 -> x0, local copies, waits for them, and re-layouts: 153 us -> none  [the longest x5 146 us: on_device(): partial_scores = jnp.take_along_axis(picked, cand_offset, axis=2)]
    pallas_call x0 -> x1, Pallas kernels: none -> 121 us  [on_device(): pl.pallas_call(step_kernel, out_shape=(jax.ShapeDtypeStruct((1, 128), F32...]
    scatter x2 -> x0, local copies, waits for them, and re-layouts: 117 us -> none  [the longest x1 113 us: on_device(): jnp.zeros((slot_total * ROWS,), jnp.bfloat16).at[flat_index]]
    all_to_all x2 -> x0, blocking collectives: 35.1 us -> none  [the longest x1 21.4 us: on_device(): lax.all_to_all(block_part, 'corpus', split_axis=0, concat_axis=0, tiled=T...]
    all_to_all x2 -> x0, waiting for transfers between devices: 32.4 us -> none  [the longest x1 24 us: on_device(): lax.all_to_all(send_queries, 'corpus', split_axis=0, concat_axis=0, tiled...]
    reduce_scatter x1 -> x0, waiting for transfers between devices: 31 us -> none  [on_device(): lax.psum_scatter(lax.dot_general(columns, query_grad, (((0,), (0,)), ((),...]
    all_gather x1 -> x0, waiting for transfers between devices: 25.5 us -> none  [on_device(): lax.all_gather(head_weight, 'fsdp', axis=0, tiled=True)]
  transfers between devices with their start and end apart: 6 -> 0, of which waited for: 6 -> 0; matrix products, arithmetic and copies ran while one was open for 1% -> 0% of each run, Pallas kernels for 0% -> 0%
where the time goes in v2:
time: 129 us
  Pallas kernels  121 us (94%)
  other arithmetic  6.63 us (5%)
    pallas_call x1, Pallas kernels, on_device(): pl.pallas_call(step_kernel, out_shape=(jax.ShapeDtypeStruct((1, 128), F32...  121 us
    convert_element_type x1, other arithmetic, on_device(): return (kl.reshape(128), hg.astype(F32))  6.63 us

profile of v2, /device:TPU:1, one launch (start us, length us, event | category | flops | bytes accessed | tf_op | source)
XLA Modules:
  0.0 129.1 jit_solution(13709619278984038140)
XLA Ops:
  0.6 121.3 %shard_map.86 = (f32[1,128]{1,0:T(1,128)}, bf16[2048,1024]{1,0:T(8,128)(2,1)}) custom-call(bf16[128,4096]{1,0:T(8,128)(2,1)} %x_hbm.1, bf16[2048,1024]{1,0:T(8,128)(2,1)} %w_hbm.1, bf16[1024,1024]{1,0:T(8,128)(2,1)} %p_hbm.1, f32[128,128]{1,0:T(8,128)} %bitcast.9, s32[128,128]{1,0:T(8,128)} %bitcast.10, s32[4,128]{1,0:T(4,128)} %bitcast.11, s32[1,128]{1,0:T(1,128)} %bitcast.12), custom_call_target="tpu_custom_call" | custom-call | tf_op jit(solution)/shard_map/pallas_call | solution.py:527
  122.0 0.0 copy-start
  122.0 6.6 %convert_element_type.3 = f32[2048,1024]{1,0:T(8,128)} convert(bf16[2048,1024]{1,0:T(8,128)(2,1)} %get-tuple-element.5) | non-fusion elementwise | flops 2097152 | bytes 12582912 | tf_op jit(solution)/shard_map/convert_element_type | solution.py:554
  128.6 0.0 copy-done
  128.6 0.5 copy.10
Async XLA Ops:
  122.0 6.6 %copy-start = (f32[1,128]{1,0:T(1,128)S(1)}, f32[1,128]{1,0:T(1,128)}, u32[]{:S(2)}) copy-start(f32[1,128]{1,0:T(1,128)} %get-tuple-element.4) | copy-start | bytes 1540

commit v3 on v2

--- a/solution.py
+++ b/solution.py
@@ -12,6 +12,7 @@
 SLOTS = 48
 ALL = 768
 LANES = 128
+VLIM = 62_816_256
 HALF = 512
 MESH = pl.DeviceIdType.MESH
 FAR = ((2, 2), (1, 2), (2, 1), (3, 2), (2, 3), (1, 1), (3, 3), (1, 3), (3, 1),
@@ -92,6 +93,20 @@
     for g in range(4):
         rank = jnp.sum(jnp.where(slots[g] == row, before, 0.0), axis=0, keepdims=True).astype(I32)
         places.append((slots[g] >> 3) * SLOTS + rank * 8 + (slots[g] & 7))
+    pl.semaphore_wait(barrier, 19)
+
+    def fs_copy(src, dst, k):
+        return pltpu.make_async_remote_copy(
+            src_ref=src, dst_ref=dst, send_sem=fs_send.at[k], recv_sem=fs_recv.at[k],
+            device_id={"fsdp": 1 - f}, device_id_type=MESH)
+
+    def begin(copy):
+        copy.start()
+        sent.append(copy)
+        return copy
+
+    swap_x = begin(fs_copy(x_hbm.at[:, other_cols], xcat.at[pl.ds(128, 128), :], 0))
+
     for n in range(4):
         place_row = lax.broadcasted_iota(I32, (192, LANES), 0) + n * 192
         total = jnp.zeros((192, LANES), F32)
@@ -101,20 +116,6 @@
             pm[n * 192:(n + 1) * 192, g * 128:(g + 1) * 128] = one.astype(BF)
         r[n * 192:(n + 1) * 192, :] = total.astype(BF)
 
-    pl.semaphore_wait(barrier, 19)
-
-    def fs_copy(src, dst, k):
-        return pltpu.make_async_remote_copy(
-            src_ref=src, dst_ref=dst, send_sem=fs_send.at[k], recv_sem=fs_recv.at[k],
-            device_id={"fsdp": 1 - f}, device_id_type=MESH)
-
-    def begin(copy):
-        copy.start()
-        sent.append(copy)
-        return copy
-
-    swap_x = begin(fs_copy(x_hbm.at[:, other_cols], xcat.at[pl.ds(128, 128), :], 0))
-
     def view(ref, at, h):
         rows = pl.ds(pl.multiple_of(at * SLOTS, 16), SLOTS)
         return ref.at[rows, :] if h is None else ref.at[rows, half_cols(h)]
@@ -185,25 +186,6 @@
             def _(n, src=src, dst=dst, chan=chan, h=h):
                 out_copy(src, dst, chan, h, lax.div(n, SIDE), lax.rem(n, SIDE)).wait_send()
 
-    load_x.wait()
-    load_w.wait()
-
-    @pl.loop(0, 4)
-    def _(n):
-        cols = pl.ds(pl.multiple_of(n * 256, 256), 256)
-        part_own[:, cols] = dot(xcat[0:128, :], w[:, cols])
-
-    swap_x.wait_recv()
-    swaps = []
-    for h in range(2):
-        @pl.loop(2 * h, 2 * h + 2)
-        def _(n):
-            cols = pl.ds(pl.multiple_of(n * 256, 256), 256)
-            part_send[:, cols] = dot(xcat[128:256, :], w[:, cols])
-
-        swaps.append(begin(fs_copy(
-            part_send.at[:, half_cols(h)], part_recv.at[:, half_cols(h)], 1 + h)))
-
     def along(half, stage, i):
         if (half == 0) == (stage == 0):
             there = lax.rem(z + i, SIDE)
@@ -222,9 +204,24 @@
         return remote(xcat.at[:, cols], xz.at[half, i - 1],
                       xb_send.at[half, i - 1], xb_recv.at[half, i - 1], dev)
 
+    load_x.wait()
+    swap_x.wait_recv()
     for i in (2, 1, 3):
         for half in range(2):
             begin(xb_copy(half, i))
+
+    load_w.wait()
+    swaps = []
+    for h in range(2):
+        @pl.loop(2 * h, 2 * h + 2)
+        def _(n):
+            cols = pl.ds(pl.multiple_of(n * 256, 256), 256)
+            rows = dot(xcat[...], w[:, cols])
+            part_own[:, cols] = rows[0:128, :]
+            part_send[:, cols] = rows[128:256, :]
+
+        swaps.append(begin(fs_copy(
+            part_send.at[:, half_cols(h)], part_recv.at[:, half_cols(h)], 1 + h)))
 
     for h in range(2):
         cols = half_cols(h)
@@ -526,7 +523,7 @@
     dma = pltpu.SemaphoreType.DMA
     kl, hg = pl.pallas_call(
         step_kernel,
-        out_shape=(jax.ShapeDtypeStruct((1, 128), F32), jax.ShapeDtypeStruct((2048, 1024), BF)),
+        out_shape=(jax.ShapeDtypeStruct((1, 128), F32), pltpu.VMEM((2048, 1024), BF)),
         in_specs=[anywhere, anywhere, anywhere, vmem, vmem, vmem, vmem],
         out_specs=(vmem, vmem),
         scratch_shapes=[
@@ -548,7 +545,7 @@
             dma((2, 2, 4, 3)), dma((2, 2, 4, 3)),
         ],
         compiler_params=pltpu.CompilerParams(
-            collective_id=0, has_side_effects=True, vmem_limit_bytes=56 * 1024 * 1024),
+            collective_id=0, has_side_effects=True, vmem_limit_bytes=VLIM),
     )(queries_in, head_weight, passages, teacher.reshape(128, 128).T,
       cand_offset.reshape(128, 128).T, cand_block.T, block_slot.reshape(1, 128))
     return kl.reshape(128), hg.astype(F32)

time: 129 us -> 125 us (0.969)
  other arithmetic: 6.63 us -> 4.44 us
  Pallas kernels: 121 us -> 119 us
    convert_element_type x1, other arithmetic: 6.63 us -> 4.44 us  [on_device(): return (kl.reshape(128), hg.astype(F32))]
    pallas_call x1, Pallas kernels: 121 us -> 119 us  [on_device(): pl.pallas_call(step_kernel, out_shape=(jax.ShapeDtypeStruct((1, 128), F32...]
where the time goes in v3:
time: 125 us
  Pallas kernels  119 us (95%)
  other arithmetic  4.44 us (4%)
    pallas_call x1, Pallas kernels, on_device(): pl.pallas_call(step_kernel, out_shape=(jax.ShapeDtypeStruct((1, 128), F32...  119 us
    convert_element_type x1, other arithmetic, on_device(): return (kl.reshape(128), hg.astype(F32))  4.44 us

profile of v3, /device:TPU:1, one launch (start us, length us, event | category | flops | bytes accessed | tf_op | source)
XLA Modules:
  0.0 125.0 jit_solution(5220991579761535731)
XLA Ops:
  0.6 119.4 %shard_map.86 = (f32[1,128]{1,0:T(1,128)}, bf16[2048,1024]{1,0:T(8,128)(2,1)S(1)}) custom-call(bf16[128,4096]{1,0:T(8,128)(2,1)} %x_hbm.1, bf16[2048,1024]{1,0:T(8,128)(2,1)} %w_hbm.1, bf16[1024,1024]{1,0:T(8,128)(2,1)} %p_hbm.1, f32[128,128]{1,0:T(8,128)} %bitcast.9, s32[128,128]{1,0:T(8,128)} %bitcast.10, s32[4,128]{1,0:T(4,128)} %bitcast.11, ...), custom_call_target="tpu_custom_call" | custom-call | tf_op jit(solution)/shard_map/pallas_call | solution.py:524
  120.0 0.0 copy-start
  120.0 4.4 %convert_element_type.3 = f32[2048,1024]{1,0:T(8,128)} convert(bf16[2048,1024]{1,0:T(8,128)(2,1)S(1)} %get-tuple-element.5) | non-fusion elementwise | flops 2097152 | bytes 12582912 | tf_op jit(solution)/shard_map/convert_element_type | solution.py:551
  124.5 0.0 copy-done
  124.5 0.5 copy.10
Async XLA Ops:
  120.0 4.5 %copy-start = (f32[1,128]{1,0:T(1,128)S(1)}, f32[1,128]{1,0:T(1,128)}, u32[]{:S(2)}) copy-start(f32[1,128]{1,0:T(1,128)} %get-tuple-element.4) | copy-start | bytes 1540

commit v4 on v3

--- a/solution.py
+++ b/solution.py
@@ -57,11 +57,12 @@
     other_cols = pl.ds(pl.multiple_of((1 - f) * 2048, 2048), 2048)
     load_x = pltpu.make_async_copy(
         x_hbm.at[:, own_cols], xcat.at[pl.ds(0, 128), :], loc_sem.at[0])
-    load_w = pltpu.make_async_copy(w_hbm, w, loc_sem.at[1])
-    load_p = pltpu.make_async_copy(p_hbm, p, loc_sem.at[2])
+    load_w = [pltpu.make_async_copy(
+        w_hbm.at[:, half_cols(h)], w.at[:, half_cols(h)], loc_sem.at[1 + h]) for h in range(2)]
+    load_p = pltpu.make_async_copy(p_hbm, p, loc_sem.at[3])
     load_x.start()
-    load_w.start()
-    load_p.start()
+    load_w[0].start()
+    load_w[1].start()
 
     barrier = pltpu.get_barrier_semaphore()
     pl.semaphore_signal(barrier, inc=1, device_id={"fsdp": 1 - f}, device_id_type=MESH)
@@ -93,20 +94,6 @@
     for g in range(4):
         rank = jnp.sum(jnp.where(slots[g] == row, before, 0.0), axis=0, keepdims=True).astype(I32)
         places.append((slots[g] >> 3) * SLOTS + rank * 8 + (slots[g] & 7))
-    pl.semaphore_wait(barrier, 19)
-
-    def fs_copy(src, dst, k):
-        return pltpu.make_async_remote_copy(
-            src_ref=src, dst_ref=dst, send_sem=fs_send.at[k], recv_sem=fs_recv.at[k],
-            device_id={"fsdp": 1 - f}, device_id_type=MESH)
-
-    def begin(copy):
-        copy.start()
-        sent.append(copy)
-        return copy
-
-    swap_x = begin(fs_copy(x_hbm.at[:, other_cols], xcat.at[pl.ds(128, 128), :], 0))
-
     for n in range(4):
         place_row = lax.broadcasted_iota(I32, (192, LANES), 0) + n * 192
         total = jnp.zeros((192, LANES), F32)
@@ -116,6 +103,31 @@
             pm[n * 192:(n + 1) * 192, g * 128:(g + 1) * 128] = one.astype(BF)
         r[n * 192:(n + 1) * 192, :] = total.astype(BF)
 
+    load_x.wait()
+    for h in range(2):
+        load_w[h].wait()
+        if h == 1:
+            load_p.start()
+
+        @pl.loop(2 * h, 2 * h + 2)
+        def _(n):
+            cols = pl.ds(pl.multiple_of(n * 256, 256), 256)
+            part_own[:, cols] = dot(xcat[0:128, :], w[:, cols])
+
+    pl.semaphore_wait(barrier, 19)
+
+    def fs_copy(src, dst, k):
+        return pltpu.make_async_remote_copy(
+            src_ref=src, dst_ref=dst, send_sem=fs_send.at[k], recv_sem=fs_recv.at[k],
+            device_id={"fsdp": 1 - f}, device_id_type=MESH)
+
+    def begin(copy):
+        copy.start()
+        sent.append(copy)
+        return copy
+
+    swap_x = begin(fs_copy(x_hbm.at[:, other_cols], xcat.at[pl.ds(128, 128), :], 0))
+
     def view(ref, at, h):
         rows = pl.ds(pl.multiple_of(at * SLOTS, 16), SLOTS)
         return ref.at[rows, :] if h is None else ref.at[rows, half_cols(h)]
@@ -198,27 +210,26 @@
             src_ref=src, dst_ref=dst, send_sem=send_sem, recv_sem=recv_sem,
             device_id={"corpus": dev}, device_id_type=MESH)
 
-    def xb_copy(half, i):
+    def xb_copy(half, i, core):
         there, dev = along(half, 0, i)
         cols = pl.ds(pl.multiple_of(half * 1024 + there * 256, 256), 256)
-        return remote(xcat.at[:, cols], xz.at[half, i - 1],
-                      xb_send.at[half, i - 1], xb_recv.at[half, i - 1], dev)
-
-    load_x.wait()
-    swap_x.wait_recv()
-    for i in (2, 1, 3):
-        for half in range(2):
-            begin(xb_copy(half, i))
-
-    load_w.wait()
+        rows = pl.ds(core * 128, 128)
+        return remote(xcat.at[rows, cols], xz.at[half, i - 1, rows, :],
+                      xb_send.at[core, half, i - 1], xb_recv.at[core, half, i - 1], dev)
+
+    for core in range(2):
+        if core == 1:
+            swap_x.wait_recv()
+        for i in (2, 1, 3):
+            for half in range(2):
+                begin(xb_copy(half, i, core))
+
     swaps = []
     for h in range(2):
         @pl.loop(2 * h, 2 * h + 2)
         def _(n):
             cols = pl.ds(pl.multiple_of(n * 256, 256), 256)
-            rows = dot(xcat[...], w[:, cols])
-            part_own[:, cols] = rows[0:128, :]
-            part_send[:, cols] = rows[128:256, :]
+            part_send[:, cols] = dot(xcat[128:256, :], w[:, cols])
 
         swaps.append(begin(fs_copy(
             part_send.at[:, half_cols(h)], part_recv.at[:, half_cols(h)], 1 + h)))
@@ -372,7 +383,9 @@
         cols = pl.ds(pl.multiple_of(half * 1024 + here * 256, 256), 256)
         xzt[half, 0, :, :] = xcat[:, cols].T
         for i in (1, 3, 2):
-            wait_recv(xz.at[half, i - 1], xb_send.at[half, i - 1], xb_recv.at[half, i - 1])
+            for core in range(2):
+                wait_recv(xz.at[half, i - 1, pl.ds(core * 128, 128), :],
+                          xb_send.at[core, half, i - 1], xb_recv.at[core, half, i - 1])
             xzt[half, i, :, :] = xz[half, i - 1, :, :].T
 
     def ql_copy(src, axis, h, i, slot):
@@ -538,9 +551,9 @@
             V((ALL, 1024), BF), V((ALL, 1024), BF), V((ALL, 1024), BF),
             V((128, 1024), F32), V((256, 1024), BF), V((2, 3, 256, 1024), BF),
             V((2, 256, 1024), F32), V((2, 3, 64, 1024), BF), V((2, 3, 64, 1024), BF),
-            dma((3,)), dma((5,)), dma((5,)), dma((4, 2, 16)), dma((4, 2, 16)),
+            dma((4,)), dma((5,)), dma((5,)), dma((4, 2, 16)), dma((4, 2, 16)),
             dma((4,)), dma((4,)),
-            dma((2, 3)), dma((2, 3)), dma((2, 2, 3)), dma((2, 2, 3)), dma((2, 2, 3)),
+            dma((2, 2, 3)), dma((2, 2, 3)), dma((2, 2, 3)), dma((2, 2, 3)), dma((2, 2, 3)),
             dma((2, 2, 3)), dma((2, 2, 3)), dma((2, 2, 3)), dma((2, 2, 3)), dma((2, 2, 3)),
             dma((2, 2, 4, 3)), dma((2, 2, 4, 3)),
         ],

time: 125 us -> 120 us (0.960)
  Pallas kernels: 119 us -> 115 us
    pallas_call x1, Pallas kernels: 119 us -> 115 us  [on_device(): pl.pallas_call(step_kernel, out_shape=(jax.ShapeDtypeStruct((1, 128), F32...]
where the time goes in v4:
time: 120 us
  Pallas kernels  115 us (96%)
  other arithmetic  4.44 us (4%)
    pallas_call x1, Pallas kernels, on_device(): pl.pallas_call(step_kernel, out_shape=(jax.ShapeDtypeStruct((1, 128), F32...  115 us
    convert_element_type x1, other arithmetic, on_device(): return (kl.reshape(128), hg.astype(F32))  4.44 us

profile of v4, /device:TPU:1, one launch (start us, length us, event | category | flops | bytes accessed | tf_op | source)
XLA Modules:
  0.0 120.1 jit_solution(2117190974802919318)
XLA Ops:
  0.6 114.5 %shard_map.86 = (f32[1,128]{1,0:T(1,128)}, bf16[2048,1024]{1,0:T(8,128)(2,1)S(1)}) custom-call(bf16[128,4096]{1,0:T(8,128)(2,1)} %x_hbm.1, bf16[2048,1024]{1,0:T(8,128)(2,1)} %w_hbm.1, bf16[1024,1024]{1,0:T(8,128)(2,1)} %p_hbm.1, f32[128,128]{1,0:T(8,128)} %bitcast.9, s32[128,128]{1,0:T(8,128)} %bitcast.10, s32[4,128]{1,0:T(4,128)} %bitcast.11, ...), custom_call_target="tpu_custom_call" | custom-call | tf_op jit(solution)/shard_map/pallas_call | solution.py:537
  115.2 0.0 copy-start
  115.2 4.4 %convert_element_type.3 = f32[2048,1024]{1,0:T(8,128)} convert(bf16[2048,1024]{1,0:T(8,128)(2,1)S(1)} %get-tuple-element.5) | non-fusion elementwise | flops 2097152 | bytes 12582912 | tf_op jit(solution)/shard_map/convert_element_type | solution.py:564
  119.6 0.0 copy-done
  119.6 0.5 copy.10
Async XLA Ops:
  115.2 4.5 %copy-start = (f32[1,128]{1,0:T(1,128)S(1)}, f32[1,128]{1,0:T(1,128)}, u32[]{:S(2)}) copy-start(f32[1,128]{1,0:T(1,128)} %get-tuple-element.4) | copy-start | bytes 1540
